TPU v7x, 512 devices: a whole 4x4x16 slice. The times are simulated.
512 devices in a mesh: row: 32 (over x, z_lo, core), col: 16 (over y, z_hi).
Axes of the slice: x: 4, y: 4, z: 16 (z_hi: 4, z_lo: 4; z = z_hi * 4 + z_lo), core: 2. Of those that a mesh axis runs over, the one named last changes fastest.
Arguments:
- hidden_img: bfloat16 [16384, 2432], P('row', 'col'), may hold values from -75 to 75
- hidden_txt: bfloat16 [3072, 2432], P('row', 'col'), may hold values from -75 to 75
- text_len: int32 [16], replicated, may hold values from 1 to 154, as said below
- step_index: int32 [16], replicated, may hold values from 0 to 27
- latent: float32 [16384, 64], P('row'), may hold values from -6 to 6
- cond: float32 [16, 2432], P(None, 'row'), may hold values from -6 to 6
- mod_weight: bfloat16 [2432, 7, 2432], P('row', None, 'col'), may hold values from -0.125 to 0.125
- qkv_weight: bfloat16 [2432, 3, 2048], P('row', None, 'col'), may hold values from -0.125 to 0.125
- kv_text_weight: bfloat16 [2432, 2, 2048], P('row', None, 'col'), may hold values from -0.125 to 0.125
- q_gain: float32 [64], replicated, may hold values from 0.5 to 6
- k_gain: float32 [2, 64], replicated, may hold values from 0.5 to 6
- out_weight: bfloat16 [2048, 2432], P('row', 'col'), may hold values from -6 to 6
- final_weight: bfloat16 [2432, 64], P('row'), may hold values from -0.125 to 0.125
Outputs:
- velocity: float32 [16384, 64], P('row')
- latent_next: float32 [16384, 64], P('row')
Inputs may be any that keep to these rules, and one draw needn't show every extreme that they name: `text_len`: some request has exactly 154 text tokens in every draw.
All inputs are finite; a program needn't handle non-finite values.
Results may differ from a plain program's by a relative error of at most 0.015.
The roundings to bfloat16 on the way count: a program that leaves them out, or rounds other values in their place, can miss the bound.
Values may be sent and summed in bfloat16 or wider, within the bound.
A program may use at most 64 MiB of HBM per device.

v0:
```python
import jax
import jax.numpy as jnp
from jax import lax
from jax.sharding import PartitionSpec as P

STEPS = 28
EPS_NORM = 1e-06


def partner_2(block, axis, distance):
    count = lax.axis_size(axis)
    route = []
    for low in range(count):
        high = low | 1 << distance
        if high != low and high < count:
            route += [(low, high), (high, low)]
    return lax.ppermute(block, axis, route)


def modulate_full(values, offset, stretch):
    average = jnp.mean(values, axis=1, keepdims=True)
    mean_square = jnp.mean(values * values, axis=1, keepdims=True)
    normed = (values - average) * lax.rsqrt(mean_square - average * average + EPS_NORM)
    return (normed * (1.0 + stretch) + offset).astype(jnp.bfloat16)


def head_norm(values, gain_row):
    mean_square = jnp.mean(values * values, axis=-1, keepdims=True)
    return (values * lax.rsqrt(mean_square + EPS_NORM) * gain_row).astype(jnp.bfloat16)


def sigma_of(step_now):
    remain = 1.0 - step_now.astype(jnp.float32) / STEPS
    return 3.0 * remain / (1.0 + 2.0 * remain)


def per_device(
    hidden_img,
    hidden_txt,
    text_len,
    step_index,
    latent,
    cond,
    mod_weight,
    qkv_weight,
    kv_text_weight,
    q_gain,
    k_gain,
    out_weight,
    final_weight,
):
    row_pos = lax.axis_index("row")
    request = row_pos // 2
    lower_half = row_pos % 2 == 0
    img_rows, width_part = hidden_img.shape
    txt_rows = hidden_txt.shape[0]
    head_dim = q_gain.shape[0]
    qkv_cols = qkv_weight.shape[2]
    heads_here = qkv_cols // head_dim
    activated = jax.nn.silu(cond).astype(jnp.bfloat16)
    mod_local = mod_weight.reshape(mod_weight.shape[0], 7 * width_part)
    mod_terms = jnp.dot(activated, mod_local, preferred_element_type=jnp.float32).reshape(
        activated.shape[0], 7, width_part
    )
    mod_all = lax.psum(mod_terms, "row")
    mod_own = lax.dynamic_index_in_dim(mod_all, request, 0, keepdims=False)
    mod_full = lax.all_gather(mod_own, "col", axis=1, tiled=True)
    img_full, txt_full = (
        lax.all_gather(hidden_img, "col", axis=1, tiled=True),
        lax.all_gather(hidden_txt, "col", axis=1, tiled=True),
    )
    img_ready = modulate_full(img_full.astype(jnp.float32), mod_full[0], mod_full[1])
    txt_ready = modulate_full(txt_full.astype(jnp.float32), mod_full[3], mod_full[4])
    qkv_flat = qkv_weight.reshape(qkv_weight.shape[0], 3 * qkv_cols)
    kv_flat = kv_text_weight.reshape(kv_text_weight.shape[0], 2 * qkv_cols)
    img_proj = jnp.dot(
        img_ready,
        lax.all_gather(qkv_flat, "row", axis=0, tiled=True),
        preferred_element_type=jnp.float32,
    )
    txt_proj = jnp.dot(
        txt_ready,
        lax.all_gather(kv_flat, "row", axis=0, tiled=True),
        preferred_element_type=jnp.float32,
    )
    img_proj = img_proj.reshape(img_rows, 3, heads_here, head_dim)
    txt_proj = txt_proj.reshape(txt_rows, 2, heads_here, head_dim)
    queries = head_norm(img_proj[:, 0], q_gain)
    img_keys = head_norm(img_proj[:, 1], k_gain[0])
    img_values = img_proj[:, 2].astype(jnp.bfloat16)
    txt_keys = head_norm(txt_proj[:, 0], k_gain[1])
    txt_values = txt_proj[:, 1].astype(jnp.bfloat16)
    length = lax.dynamic_index_in_dim(text_len, request, 0, keepdims=False)
    scaling = head_dim ** (-0.5)
    partner = partner_2((img_keys, img_values, txt_keys, txt_values), "row", 0)

    def ordered(own_part, peer_part):
        return jnp.concatenate(
            [
                jnp.where(lower_half, own_part, peer_part),
                jnp.where(lower_half, peer_part, own_part),
            ],
            axis=0,
        )

    all_keys = jnp.concatenate(
        [ordered(img_keys, partner[0]), ordered(txt_keys, partner[2])], axis=0
    )
    all_values = jnp.concatenate(
        [ordered(img_values, partner[1]), ordered(txt_values, partner[3])], axis=0
    )
    key_valid = jnp.concatenate(
        [jnp.ones((2 * img_rows,), dtype=bool), jnp.arange(2 * txt_rows) < length]
    )

    def attend(head_ops):
        q_head, k_head, v_head = head_ops
        scores = jnp.dot(q_head, k_head.T, preferred_element_type=jnp.float32) * scaling
        scores = jnp.where(key_valid[None, :], scores, -jnp.inf)
        row_max = jnp.max(scores, axis=1, keepdims=True)
        weights = jnp.exp(scores - row_max)
        probabilities = (weights / jnp.sum(weights, axis=1, keepdims=True)).astype(jnp.bfloat16)
        return jnp.dot(probabilities, v_head, preferred_element_type=jnp.float32).astype(
            jnp.bfloat16
        )

    attended = lax.map(
        attend,
        (jnp.moveaxis(queries, 1, 0), jnp.moveaxis(all_keys, 1, 0), jnp.moveaxis(all_values, 1, 0)),
    )
    attended = jnp.moveaxis(attended, 0, 1).reshape(img_rows, qkv_cols)
    full_heads = lax.all_gather(attended, "col", axis=1, tiled=True)
    projected = jnp.dot(
        full_heads,
        lax.all_gather(out_weight, "row", axis=0, tiled=True),
        preferred_element_type=jnp.float32,
    )
    updated = (hidden_img.astype(jnp.float32) + mod_own[2] * projected).astype(jnp.bfloat16)
    head_full = lax.all_gather(final_weight, "row", axis=0, tiled=True)
    residual = lax.all_gather(updated, "col", axis=1, tiled=True)
    head_in = modulate_full(residual.astype(jnp.float32), mod_full[5], mod_full[6])
    velocity = jnp.dot(head_in, head_full, preferred_element_type=jnp.float32)
    step_now = lax.dynamic_index_in_dim(step_index, request, 0, keepdims=False)
    sigma_step = sigma_of(step_now + 1) - sigma_of(step_now)
    latent_next = latent + sigma_step * velocity
    return (velocity, latent_next)


def solution(mesh):
    in_specs = (
        P("row", "col"),
        P("row", "col"),
        P(),
        P(),
        P("row", None),
        P(None, "row"),
        P("row", None, "col"),
        P("row", None, "col"),
        P("row", None, "col"),
        P(),
        P(),
        P("row", "col"),
        P("row", None),
    )
    out_specs = (P("row", None), P("row", None))
    return jax.shard_map(
        per_device, mesh=mesh, in_specs=in_specs, out_specs=out_specs, check_vma=False
    )
```

profile of v0, /device:TPU:1, one launch (start us, length us, event | category | flops | bytes accessed | tf_op | source)
XLA Modules:
  0.0 753.6 jit_solution(9680876865259763626)
XLA Ops:
  7.2 0.0 all-reduce.3.cloned.1.call-start
  7.2 0.9 copy-done
  8.1 1.6 fusion.48
  9.7 0.0 all-reduce.3.cloned.1.call-update
  9.8 0.0 all-gather.18.cloned.1.call-start
  9.8 1.4 reshape.166
  11.2 0.0 all-gather.18.cloned.1.call-update
  11.3 0.0 all-gather.16.cloned.1.call-start
  11.3 0.9 copy.53
  12.2 0.7 reshape.164
  12.9 0.0 all-gather.16.cloned.1.call-update
  12.9 0.0 all-gather.10.cloned.1.call-start
  12.9 0.5 all-gather.10.cloned.1.call-update
  13.5 0.0 all-gather.12.cloned.1.call-start
  13.6 1.2 dynamic_slice.23
  14.8 0.6 iota_compare_fusion
  15.4 61.1 %all_gather.30 = bf16[96,2432]{0,1:T(8,128)(2,1)S(1)} all-gather(bf16[96,152]{0,1:T(8,128)(2,1)} %param.16), channel_id=1, replica_groups=mesh['row'=32,'col'=16] {'col'}, dimensions={1}, use_global_device_ids=true | all-gather | bytes 496128 | tf_op jit(solution)/shard_map/all_gather | solution.py:70
  76.5 0.3 convert_reduce_fusion.2
  76.8 1.3 slice_bitcast_fusion.3
  78.1 199.8 %all-reduce.3.cloned.1.call-done = f32[16,7,152]{2,0,1:T(8,128)} async-done(((f32[16,7,152]{2,0,1:T(8,128)}), f32[16,7,152]{2,0,1:T(8,128)}) %all-reduce.3.cloned.1.call-update) | async-done | bytes 68112 | tf_op jit(solution)/shard_map/psum | solution.py:65
  277.9 0.8 constant_dynamic-slice_fusion.1
  278.7 0.1 copy.52
  278.8 77.3 %all-gather = f32[1,7,2432]{1,0,2:T(1,128)S(1)} all-gather(f32[1,7,152]{1,0,2:T(1,128)S(1)} %copy.52), channel_id=2, replica_groups=mesh['row'=32,'col'=16] {'col'}, dimensions={2}, use_global_device_ids=true | all-gather | bytes 72352 | tf_op jit(solution)/shard_map/all_gather | solution.py:67
  356.1 42.9 %fusion.39 = (f32[2432]{0:T(1024)}, f32[2432]{0:T(1024)S(1)}, f32[2432]{0:T(1024)S(1)}, f32[2432]{0:T(1024)}, f32[2432]{0:T(1024)}, /*index=5*/f32[2432]{0:T(1024)}) fusion(f32[1,7,2432]{1,0,2:T(1,128)S(1)} %all-gather), kind=kLoop, calls=%fused_computation.55 | loop fusion | flops 7296 | bytes 116736 | tf_op jit(solution)/shard_map/add | solution.py:24
  399.0 2.2 reshape.167
  401.1 1.3 fusion.42
  402.4 6.7 collective-permute-start.3
  409.2 0.1 multiply_convert_fusion.2
  409.2 1.9 collective-permute-start.1
  411.2 0.6 broadcast_select_fusion.4
  411.8 0.5 collective-permute-done.1
  412.3 0.7 broadcast_select_fusion.6
  413.1 14.4 %all-gather.16.cloned.1.call-done = bf16[32,76,384]{2,1,0:T(8,128)(2,1)} async-done(((bf16[1,76,384]{2,1,0:T(8,128)(2,1)}), bf16[32,76,384]{2,1,0:T(8,128)(2,1)}) %all-gather.16.cloned.1.call-update) | async-done | bytes 1867792 | tf_op jit(solution)/shard_map/all_gather | solution.py:78
  427.5 2.5 reshape.165
  429.9 103.8 %all-gather.10.cloned.1.call-done = bf16[512,2432]{0,1:T(8,128)(2,1)} async-done(((bf16[512,152]{0,1:T(8,128)(2,1)}), bf16[512,2432]{0,1:T(8,128)(2,1)}) %all-gather.10.cloned.1.call-update) | async-done | bytes 2490384 | tf_op jit(solution)/shard_map/all_gather | solution.py:69
  533.7 2.6 convert_reduce_fusion.1
  536.4 1.9 fusion.24
  538.3 0.1 multiply_reduce_fusion
  538.4 0.1 multiply_convert_fusion
  538.5 2.8 collective-permute-start
  541.3 2.1 collective-permute-start.2
  543.5 0.9 concatenate.10
  544.4 0.4 collective-permute-done.2
  544.8 0.1 concatenate.11
  544.9 3.1 while.10
  544.9 0.5 fusion.66
  545.5 0.4 fusion.67
  545.9 0.6 fusion.68
  546.5 0.6 fusion.66
  547.0 0.4 fusion.67
  547.4 0.6 fusion.68
  548.0 0.6 copy-done.4
  548.7 0.0 all-gather.14.cloned.1.call-start
  548.7 44.3 %all_gather.33 = bf16[2048,152]{1,0:T(8,128)(2,1)S(1)} all-gather(bf16[64,152]{1,0:T(8,128)(2,1)S(1)} %copy-done.6), channel_id=1, replica_groups=mesh['row'=32,'col'=16] {'row'}, dimensions={0}, use_global_device_ids=true | all-gather | bytes 642048 | tf_op jit(solution)/shard_map/all_gather | solution.py:135
  593.1 0.7 constant_dynamic-slice_fusion
  593.8 45.6 %all-gather.12.cloned.1.call-done = bf16[512,2048]{0,1:T(8,128)(2,1)} async-done(((bf16[512,128]{0,1:T(8,128)(2,1)}), bf16[512,2048]{0,1:T(8,128)(2,1)}) %all-gather.12.cloned.1.call-update) | async-done | bytes 2097168 | tf_op jit(solution)/shard_map/all_gather | solution.py:132
  639.4 2.8 fusion.41
  642.3 0.6 dynamic_slice.24
  644.2 45.2 %all-gather.3 = bf16[32,76,64]{1,2,0:T(8,128)(2,1)S(1)} all-gather(bf16[1,76,64]{1,2,0:T(8,128)(2,1)S(1)} %bitcast.104), channel_id=1, replica_groups=mesh['row'=32,'col'=16] {'row'}, dimensions={0}, use_global_device_ids=true | all-gather | bytes 321024 | tf_op jit(solution)/shard_map/all_gather | solution.py:139
  689.4 0.3 copy.58
  689.8 0.8 reshape.169
  690.6 51.6 %all-gather.14.cloned.1.call-done = bf16[512,2432]{0,1:T(8,128)(2,1)} async-done(((bf16[512,152]{0,1:T(8,128)(2,1)}), bf16[512,2432]{0,1:T(8,128)(2,1)}) %all-gather.14.cloned.1.call-update) | async-done | bytes 2490384 | tf_op jit(solution)/shard_map/all_gather | solution.py:140
  742.3 2.6 convert_reduce_fusion
  744.9 1.8 multiply_add_fusion
  (47 shorter events, 0.3 us)
Async XLA Ops:
  7.2 1.0 copy-start
  7.2 270.7 %all-reduce.3.cloned.1.call-start = ((), (), s32[]{:S(2)}) async-start(), calls=%async_computation | async-start | bytes 229376 | tf_op jit(solution)/shard_map/psum | solution.py:65
  9.8 389.2 %all-gather.18.cloned.1.call-start = ((), (), s32[]{:S(2)}) async-start(), calls=%async_computation.5 | async-start | bytes 1351680 | tf_op jit(solution)/shard_map/all_gather | solution.py:83
  11.3 416.2 %all-gather.16.cloned.1.call-start = ((), (), s32[]{:S(2)}) async-start(), calls=%async_computation.4 | async-start | bytes 2027520 | tf_op jit(solution)/shard_map/all_gather | solution.py:78
  12.9 520.9 %all-gather.10.cloned.1.call-start = ((), (), s32[]{:S(2)}) async-start(), calls=%async_computation.1 | async-start | bytes 2646016 | tf_op jit(solution)/shard_map/all_gather | solution.py:69
  13.5 626.0 %all-gather.12.cloned.1.call-start = ((), (), s32[]{:S(2)}) async-start(), calls=%async_computation.2 | async-start | bytes 2228224 | tf_op jit(solution)/shard_map/all_gather | solution.py:132
  402.4 8.8 %collective-permute-start.3 = (bf16[96,2,64]{0,2,1:T(8,128)(2,1)S(1)}, bf16[96,2,64]{0,2,1:T(8,128)(2,1)S(1)}, u32[]{:S(2)}, u32[]{:S(2)}) collective-permute-start(bf16[96,2,64]{0,2,1:T(8,128)(2,1)S(1)} %fusion.52), channel_id=1, source_target_pairs={{0,16},{16,0},{32,48},{48,32},{64,80},{80,64},{96,112},{112,96},{1... | collective-permute-start | bytes 73736 | tf_op jit(solution)/shard_map/ppermute | solution.py:17
  409.2 3.1 collective-permute-start.1
  413.1 123.3 %copy-start.10 = (f32[2432]{0:T(1024)S(1)}, f32[2432]{0:T(1024)}, u32[]{:S(2)}) copy-start(f32[2432]{0:T(1024)} %get-tuple-element.48) | copy-start | bytes 29188
  413.1 123.3 %copy-start.11 = (f32[2432]{0:T(1024)S(1)}, f32[2432]{0:T(1024)}, u32[]{:S(2)}) copy-start(f32[2432]{0:T(1024)} %get-tuple-element.49) | copy-start | bytes 29188
  533.7 2.6 copy-start.1
  536.3 2.0 copy-start.12
  536.3 2.0 copy-start.13
  538.2 6.5 copy-start.5
  538.5 5.0 collective-permute-start
  541.3 3.4 collective-permute-start.2
  544.9 3.8 copy-start.6
  544.9 94.5 %copy-start.3 = (bf16[512,152]{0,1:T(8,128)(2,1)S(1)}, bf16[512,152]{0,1:T(8,128)(2,1)}, u32[]{:S(2)}) copy-start(bf16[512,152]{0,1:T(8,128)(2,1)} %param.15) | copy-start | bytes 466948
  548.0 0.7 copy-start.4
  548.0 94.3 %copy-start.15 = (s32[16]{0:T(128)S(1)}, s32[16]{0:T(128)}, u32[]{:S(2)}) copy-start(s32[16]{0:T(128)} %param.18) | copy-start | bytes 196
  548.0 96.2 %copy-start.7 = (bf16[76,64]{0,1:T(8,128)(2,1)S(1)}, bf16[76,64]{0,1:T(8,128)(2,1)}, u32[]{:S(2)}) copy-start(bf16[76,64]{0,1:T(8,128)(2,1)} %param.27) | copy-start | bytes 29188
  548.7 193.6 %all-gather.14.cloned.1.call-start = ((), (), s32[]{:S(2)}) async-start(), calls=%async_computation.3 | async-start | bytes 2646016 | tf_op jit(solution)/shard_map/all_gather | solution.py:140
  642.3 102.6 %copy-start.8 = (f32[2432]{0:T(1024)S(1)}, f32[2432]{0:T(1024)}, u32[]{:S(2)}) copy-start(f32[2432]{0:T(1024)} %get-tuple-element.45) | copy-start | bytes 29188
  642.3 102.6 %copy-start.9 = (f32[2432]{0:T(1024)S(1)}, f32[2432]{0:T(1024)}, u32[]{:S(2)}) copy-start(f32[2432]{0:T(1024)} %get-tuple-element.50) | copy-start | bytes 29188
  642.3 102.6 %copy-start.14 = (f32[512,64]{0,1:T(8,128)S(1)}, f32[512,64]{0,1:T(8,128)}, u32[]{:S(2)}) copy-start(f32[512,64]{0,1:T(8,128)} %param.19) | copy-start | bytes 393220
  742.3 2.6 copy-start.2
Sparse Core Ops, SparseCore 0:
  11.5 266.3 all-reduce.2
  280.2 76.0 all-gather.17
  359.3 68.1 all-gather.15
  430.8 102.8 all-gather.9
  548.8 90.5 all-gather.11
  642.8 99.4 all-gather.13
where the time goes:
time: 754 us
  waiting for transfers between devices  417 us (55%)
  blocking collectives  228 us (30%)
  other arithmetic  51.4 us (7%)
  local copies, waits for them, and re-layouts  16 us (2%)
  between operations  15.9 us (2%)
  starting transfers between devices  13.8 us (2%)
  matrix products  11.6 us (2%)
    psum x1, waiting for transfers between devices, per_device(): mod_all = lax.psum(mod_terms, 'row')  200 us
    all_gather x1, waiting for transfers between devices, per_device(): lax.all_gather(hidden_img, 'col', axis=1, tiled=True)  104 us
    all_gather x1, blocking collectives, per_device(): mod_full = lax.all_gather(mod_own, 'col', axis=1, tiled=True)  77.3 us
    all_gather x1, blocking collectives, per_device(): lax.all_gather(hidden_txt, 'col', axis=1, tiled=True)  61.1 us
    all_gather x1, waiting for transfers between devices, per_device(): residual = lax.all_gather(updated, 'col', axis=1, tiled=True)  51.6 us
    all_gather x1, waiting for transfers between devices, per_device(): full_heads = lax.all_gather(attended, 'col', axis=1, tiled=True)  45.6 us
    all_gather x1, blocking collectives, per_device(): head_full = lax.all_gather(final_weight, 'row', axis=0, tiled=True)  45.2 us
    all_gather x1, blocking collectives, per_device(): lax.all_gather(out_weight, 'row', axis=0, tiled=True)  44.3 us
  transfers between devices with their start and end apart: 10, of which 7 were waited for; matrix products, arithmetic and copies ran while one was open for 8% of the time, Pallas kernels for 0%

commit v1 on v0

--- a/solution.py
+++ b/solution.py
@@ -62,7 +62,7 @@
     mod_terms = jnp.dot(activated, mod_local, preferred_element_type=jnp.float32).reshape(
         activated.shape[0], 7, width_part
     )
-    mod_all = lax.psum(mod_terms, "row")
+    mod_all = jnp.sum(lax.all_gather(mod_terms, "row"), axis=0)
     mod_own = lax.dynamic_index_in_dim(mod_all, request, 0, keepdims=False)
     mod_full = lax.all_gather(mod_own, "col", axis=1, tiled=True)
     img_full, txt_full = (

time: 754 us -> 622 us (0.82)
  waiting for transfers between devices: 417 us -> 232 us
  blocking collectives: 228 us -> 283 us
    psum x1 -> x0, waiting for transfers between devices: 200 us -> none  [per_device(): mod_all = lax.psum(mod_terms, 'row')]
    all_gather x1, waiting for transfers between devices: 104 us -> 0.02 us  [per_device(): lax.all_gather(hidden_img, 'col', axis=1, tiled=True)]
    all_gather x0 -> x1, waiting for transfers between devices: none -> 66.6 us  [per_device(): mod_all = jnp.sum(lax.all_gather(mod_terms, 'row'), axis=0)]
    all_gather x1, waiting for transfers between devices: 14.4 us -> 64.1 us  [per_device(): lax.all_gather(qkv_flat, 'row', axis=0, tiled=True)]
    all_gather x1, blocking collectives: 77.3 us -> 117 us  [per_device(): mod_full = lax.all_gather(mod_own, 'col', axis=1, tiled=True)]
    all_gather x1, blocking collectives: 44.3 us -> 58.2 us  [per_device(): lax.all_gather(out_weight, 'row', axis=0, tiled=True)]
    all_gather x1, waiting for transfers between devices: 0.01 us -> 7.82 us  [per_device(): lax.all_gather(kv_flat, 'row', axis=0, tiled=True)]
  transfers between devices with their start and end apart: 10 -> 10, of which waited for: 7 -> 7; matrix products, arithmetic and copies ran while one was open for 8% -> 10% of each run, Pallas kernels for 0% -> 0%
where the time goes in v1:
time: 622 us
  blocking collectives  283 us (45%)
  waiting for transfers between devices  232 us (37%)
  other arithmetic  52.4 us (8%)
  between operations  15.9 us (3%)
  starting transfers between devices  13.3 us (2%)
  local copies, waits for them, and re-layouts  13.2 us (2%)
  matrix products  11.6 us (2%)
    all_gather x1, blocking collectives, per_device(): mod_full = lax.all_gather(mod_own, 'col', axis=1, tiled=True)  117 us
    all_gather x1, waiting for transfers between devices, per_device(): mod_all = jnp.sum(lax.all_gather(mod_terms, 'row'), axis=0)  66.6 us
    all_gather x1, waiting for transfers between devices, per_device(): lax.all_gather(qkv_flat, 'row', axis=0, tiled=True)  64.1 us
    all_gather x1, blocking collectives, per_device(): lax.all_gather(hidden_txt, 'col', axis=1, tiled=True)  60.3 us
    all_gather x1, blocking collectives, per_device(): lax.all_gather(out_weight, 'row', axis=0, tiled=True)  58.2 us
    all_gather x1, waiting for transfers between devices, per_device(): residual = lax.all_gather(updated, 'col', axis=1, tiled=True)  49.2 us
    all_gather x1, blocking collectives, per_device(): head_full = lax.all_gather(final_weight, 'row', axis=0, tiled=True)  47.5 us
    add x1, other arithmetic, modulate_full(): return (normed * (1.0 + stretch) + offset).astype(jnp.bfloat16)  42.5 us
  transfers between devices with their start and end apart: 10, of which 7 were waited for; matrix products, arithmetic and copies ran while one was open for 10% of the time, Pallas kernels for 0%

profile of v1, /device:TPU:1, one launch (start us, length us, event | category | flops | bytes accessed | tf_op | source)
XLA Modules:
  0.0 621.8 jit_solution(7362403257920120968)
XLA Ops:
  7.2 0.0 all-gather.22.cloned.1.call-start
  7.2 1.4 reshape.170
  8.7 0.0 all-gather.22.cloned.1.call-update
  8.7 0.0 all-gather.20.cloned.1.call-start
  8.7 0.9 copy.53
  9.6 0.7 reshape.168
  10.3 0.0 all-gather.20.cloned.1.call-update
  10.3 0.0 all-gather.18.cloned.1.call-start
  10.4 1.6 fusion.48
  12.0 0.0 all-gather.18.cloned.1.call-update
  12.0 0.0 all-gather.12.cloned.1.call-start
  12.1 0.5 all-gather.12.cloned.1.call-update
  12.6 0.0 all-gather.14.cloned.1.call-start
  12.7 1.3 dynamic_slice.23
  14.0 0.7 iota_compare_fusion
  14.7 60.3 %all_gather.34 = bf16[96,2432]{0,1:T(8,128)(2,1)S(1)} all-gather(bf16[96,152]{0,1:T(8,128)(2,1)} %param.16), channel_id=1, replica_groups=mesh['row'=32,'col'=16] {'col'}, dimensions={1}, use_global_device_ids=true | all-gather | bytes 496128 | tf_op jit(solution)/shard_map/all_gather | solution.py:70
  75.0 0.3 convert_reduce_fusion.2
  75.3 0.8 slice_bitcast_fusion.3
  76.1 7.8 %all-gather.22.cloned.1.call-done = bf16[32,76,256]{2,1,0:T(8,128)(2,1)} async-done(((bf16[1,76,256]{2,1,0:T(8,128)(2,1)}), bf16[32,76,256]{2,1,0:T(8,128)(2,1)}) %all-gather.22.cloned.1.call-update) | async-done | bytes 1245200 | tf_op jit(solution)/shard_map/all_gather | solution.py:83
  83.9 2.9 reshape.171
  86.9 64.1 %all-gather.20.cloned.1.call-done = bf16[32,76,384]{2,1,0:T(8,128)(2,1)} async-done(((bf16[1,76,384]{2,1,0:T(8,128)(2,1)}), bf16[32,76,384]{2,1,0:T(8,128)(2,1)}) %all-gather.20.cloned.1.call-update) | async-done | bytes 1867792 | tf_op jit(solution)/shard_map/all_gather | solution.py:78
  150.9 2.5 reshape.169
  153.4 66.6 %all-gather.18.cloned.1.call-done = f32[512,7,152]{2,0,1:T(8,128)} async-done(((f32[16,7,152]{2,0,1:T(8,128)}), f32[512,7,152]{2,0,1:T(8,128)}) %all-gather.18.cloned.1.call-update) | async-done | bytes 2179088 | tf_op jit(solution)/shard_map/all_gather | solution.py:65
  220.0 2.5 reduce_sum.99
  222.5 0.1 copy.52
  222.6 116.9 %all-gather.1 = f32[1,7,2432]{1,0,2:T(1,128)S(1)} all-gather(f32[1,7,152]{1,0,2:T(1,128)S(1)} %copy.52), channel_id=3, replica_groups=mesh['row'=32,'col'=16] {'col'}, dimensions={2}, use_global_device_ids=true | all-gather | bytes 72352 | tf_op jit(solution)/shard_map/all_gather | solution.py:67
  339.4 42.5 %fusion.39 = (f32[2432]{0:T(1024)S(1)}, f32[2432]{0:T(1024)S(1)}, f32[2432]{0:T(1024)S(1)}, f32[2432]{0:T(1024)S(1)}, f32[2432]{0:T(1024)S(1)}, /*index=5*/f32[2432]{0:T(1024)S(1)}) fusion(f32[1,7,2432]{1,0,2:T(1,128)S(1)} %all-gather.1), kind=kLoop, calls=%fused_computation.55 | loop fusion | flops 7296 | bytes 116736 | tf_op jit(solution)/shard_map/add | solution.py:24
  382.0 1.3 fusion.42
  383.2 6.6 %collective-permute-start.3 = (bf16[96,2,64]{0,2,1:T(8,128)(2,1)S(1)}, bf16[96,2,64]{0,2,1:T(8,128)(2,1)S(1)}, u32[]{:S(2)}, u32[]{:S(2)}) collective-permute-start(bf16[96,2,64]{0,2,1:T(8,128)(2,1)S(1)} %fusion.52), channel_id=1, source_target_pairs={{0,16},{16,0},{32,48},{48,32},{64,80},{80,64},{96,112},{112,96},{1... | collective-permute-start | bytes 73736 | tf_op jit(solution)/shard_map/ppermute | solution.py:17
  389.9 0.1 multiply_convert_fusion.2
  390.0 2.1 collective-permute-start.1
  392.1 1.0 collective-permute-done.1
  393.1 0.1 broadcast_select_fusion.6
  393.2 0.0 all-gather.12.cloned.1.call-done
  393.2 2.6 convert_reduce_fusion.1
  395.8 1.9 fusion.24
  397.7 0.1 multiply_reduce_fusion
  397.8 2.1 collective-permute-start.2
  399.9 0.1 multiply_convert_fusion
  400.0 2.3 collective-permute-start
  402.3 0.1 concatenate.11
  402.4 0.8 collective-permute-done
  403.3 0.1 concatenate.10
  403.4 3.1 while.10
  403.4 0.6 fusion.66
  404.0 0.4 fusion.67
  404.4 0.6 fusion.68
  405.0 0.5 fusion.66
  405.5 0.4 fusion.67
  405.9 0.6 fusion.68
  406.5 0.6 copy-done.5
  407.2 0.0 all-gather.14.cloned.1.call-update
  407.2 0.0 all-gather.16.cloned.1.call-start
  407.2 58.2 %all_gather.37 = bf16[2048,152]{1,0:T(8,128)(2,1)S(1)} all-gather(bf16[64,152]{1,0:T(8,128)(2,1)S(1)} %copy-done.6), channel_id=1, replica_groups=mesh['row'=32,'col'=16] {'row'}, dimensions={0}, use_global_device_ids=true | all-gather | bytes 642048 | tf_op jit(solution)/shard_map/all_gather | solution.py:135
  465.5 42.4 %all-gather.14.cloned.1.call-done = bf16[512,2048]{0,1:T(8,128)(2,1)} async-done(((bf16[512,128]{0,1:T(8,128)(2,1)}), bf16[512,2048]{0,1:T(8,128)(2,1)}) %all-gather.14.cloned.1.call-update) | async-done | bytes 2097168 | tf_op jit(solution)/shard_map/all_gather | solution.py:132
  507.8 2.8 fusion.41
  510.7 0.0 all-gather.16.cloned.1.call-update
  510.7 0.6 dynamic_slice.24
  512.6 47.5 %all-gather.4 = bf16[32,76,64]{1,2,0:T(8,128)(2,1)S(1)} all-gather(bf16[1,76,64]{1,2,0:T(8,128)(2,1)S(1)} %bitcast.106), channel_id=1, replica_groups=mesh['row'=32,'col'=16] {'row'}, dimensions={0}, use_global_device_ids=true | all-gather | bytes 321024 | tf_op jit(solution)/shard_map/all_gather | solution.py:139
  560.2 0.3 copy.58
  560.5 0.8 reshape.173
  561.4 49.2 %all-gather.16.cloned.1.call-done = bf16[512,2432]{0,1:T(8,128)(2,1)} async-done(((bf16[512,152]{0,1:T(8,128)(2,1)}), bf16[512,2432]{0,1:T(8,128)(2,1)}) %all-gather.16.cloned.1.call-update) | async-done | bytes 2490384 | tf_op jit(solution)/shard_map/all_gather | solution.py:140
  610.6 2.6 convert_reduce_fusion
  613.2 1.8 multiply_add_fusion
  (38 shorter events, 0.3 us)
Async XLA Ops:
  7.2 3.2 copy-start
  7.2 76.8 %all-gather.22.cloned.1.call-start = ((), (), s32[]{:S(2)}) async-start(), calls=%async_computation.5 | async-start | bytes 1351680 | tf_op jit(solution)/shard_map/all_gather | solution.py:83
  8.7 142.2 %all-gather.20.cloned.1.call-start = ((), (), s32[]{:S(2)}) async-start(), calls=%async_computation.4 | async-start | bytes 2027520 | tf_op jit(solution)/shard_map/all_gather | solution.py:78
  10.3 209.7 %all-gather.18.cloned.1.call-start = ((), (), s32[]{:S(2)}) async-start(), calls=%async_computation.3 | async-start | bytes 3784704 | tf_op jit(solution)/shard_map/all_gather | solution.py:65
  12.0 381.2 %all-gather.12.cloned.1.call-start = ((), (), s32[]{:S(2)}) async-start(), calls=%async_computation | async-start | bytes 2646016 | tf_op jit(solution)/shard_map/all_gather | solution.py:69
  12.6 495.2 %all-gather.14.cloned.1.call-start = ((), (), s32[]{:S(2)}) async-start(), calls=%async_computation.1 | async-start | bytes 2228224 | tf_op jit(solution)/shard_map/all_gather | solution.py:132
  339.4 42.5 %copy-start.3 = (bf16[2432,256]{1,0:T(8,128)(2,1)S(1)}, bf16[2432,256]{1,0:T(8,128)(2,1)}, u32[]{:S(2)}) copy-start(bf16[2432,256]{1,0:T(8,128)(2,1)} %reshape.171) | copy-start | bytes 3735556
  383.2 8.9 %collective-permute-start.3 = (bf16[96,2,64]{0,2,1:T(8,128)(2,1)S(1)}, bf16[96,2,64]{0,2,1:T(8,128)(2,1)S(1)}, u32[]{:S(2)}, u32[]{:S(2)}) collective-permute-start(bf16[96,2,64]{0,2,1:T(8,128)(2,1)S(1)} %fusion.52), channel_id=1, source_target_pairs={{0,16},{16,0},{32,48},{48,32},{64,80},{80,64},{96,112},{112,96},{1... | collective-permute-start | bytes 73736 | tf_op jit(solution)/shard_map/ppermute | solution.py:17
  390.0 3.1 collective-permute-start.1
  393.2 2.6 copy-start.1
  395.8 4.1 copy-start.8
  397.8 4.5 collective-permute-start.2
  400.0 3.2 collective-permute-start
  403.4 3.9 copy-start.6
  403.4 104.4 %copy-start.4 = (bf16[512,152]{0,1:T(8,128)(2,1)S(1)}, bf16[512,152]{0,1:T(8,128)(2,1)}, u32[]{:S(2)}) copy-start(bf16[512,152]{0,1:T(8,128)(2,1)} %param.15) | copy-start | bytes 466948
  406.5 0.7 copy-start.5
  406.5 104.2 %copy-start.10 = (s32[16]{0:T(128)S(1)}, s32[16]{0:T(128)}, u32[]{:S(2)}) copy-start(s32[16]{0:T(128)} %param.18) | copy-start | bytes 196
  406.5 106.1 %copy-start.7 = (bf16[76,64]{0,1:T(8,128)(2,1)S(1)}, bf16[76,64]{0,1:T(8,128)(2,1)}, u32[]{:S(2)}) copy-start(bf16[76,64]{0,1:T(8,128)(2,1)} %param.27) | copy-start | bytes 29188
  407.2 203.4 %all-gather.16.cloned.1.call-start = ((), (), s32[]{:S(2)}) async-start(), calls=%async_computation.2 | async-start | bytes 2646016 | tf_op jit(solution)/shard_map/all_gather | solution.py:140
  510.7 102.4 %copy-start.9 = (f32[512,64]{0,1:T(8,128)S(1)}, f32[512,64]{0,1:T(8,128)}, u32[]{:S(2)}) copy-start(f32[512,64]{0,1:T(8,128)} %param.19) | copy-start | bytes 393220
  610.6 2.6 copy-start.2
Sparse Core Ops, SparseCore 0:
  10.2 73.7 all-gather.21
  86.7 64.2 all-gather.19
  153.7 66.2 all-gather.17
  222.9 127.6 all-gather.11
  407.3 100.4 all-gather.13
  510.8 99.7 all-gather.15
